TPU v7x, 256 devices: a whole 4x4x8 slice. The times are simulated.
256 devices in a mesh: req: 32 (over z, y), mdl: 8 (over x, core).
Axes of the slice: x: 4, y: 4, z: 8, core: 2. Of those that a mesh axis runs over, the one named last changes fastest.
Arguments:
- tokens: bfloat16 [8192, 2048], P('req', 'mdl'), may hold values from -6 to 6
- prefix_cache: bfloat16 [16384, 2, 2048], P('req', None, 'mdl'), may hold values from -68 to 68
- qkv_weight: bfloat16 [2048, 3, 2048], P(None, None, 'mdl'), may hold values from -0.125 to 0.125
- out_weight: bfloat16 [2048, 2048], P('mdl'), may hold values from -0.75 to 0.75
- gate_up_weight: bfloat16 [2048, 2, 4096], P(None, None, 'mdl'), may hold values from -0.125 to 0.125
- down_weight: bfloat16 [4096, 2048], P('mdl'), may hold values from -0.09375 to 0.09375
- lengths: int32 [128], replicated, may hold values from 0 to 256, as said below
- placement: int32 [128], replicated, may hold values from 0 to 31, as said below
- request_group: int32 [128], replicated, may hold values from 0 to 3
- block_owner: int32 [32], replicated, may hold values from 0 to 31, each once
- start_position: int32 [128], replicated, may hold values from 4096 to 4351
Outputs:
- out: bfloat16 [8192, 2048], P('req', 'mdl')
Inputs may be any that keep to these rules, and one draw needn't show every extreme that they name: `placement`: each index of req holds exactly 4 requests. The lengths of the requests on one index of req sum to at most 256, and to exactly 256 on some index; all lengths together sum to exactly 128 times the number of indices of req.
All inputs are finite; a program needn't handle non-finite values.
Results may differ from a plain program's by a relative error of at most 0.017.
Values may be sent and summed in bfloat16 or wider, within the bound.
A program may use at most 128 MiB of HBM per device.

v0:
```python
import math
import jax
import jax.numpy as jnp
from jax import lax
from jax.sharding import PartitionSpec as P

HD = 128
G = 4
NEG = -1e30
EPS = 1e-05


def slot_table(lengths, placement, request_group, start_position, device, capacity):
    request_count = lengths.shape[0]
    request_ids = jnp.arange(request_count, dtype=jnp.int32)
    same_device = placement[:, None] == placement[None, :]
    earlier = request_ids[None, :] < request_ids[:, None]
    before = jnp.sum(jnp.where(same_device & earlier, lengths[None, :], 0), axis=1)
    ending = before + lengths
    slot_ids = jnp.arange(capacity, dtype=jnp.int32)
    belongs = (
        (placement[None, :] == device)
        & (slot_ids[:, None] >= before[None, :])
        & (slot_ids[:, None] < ending[None, :])
    )
    occupied = jnp.any(belongs, axis=1)
    request = jnp.sum(jnp.where(belongs, request_ids[None, :], 0), axis=1)
    slot_group = jnp.where(
        occupied, jnp.sum(jnp.where(belongs, request_group[None, :], 0), axis=1), -1
    )
    first_slot = jnp.sum(jnp.where(belongs, before[None, :], 0), axis=1)
    offset = slot_ids - first_slot
    position = jnp.sum(jnp.where(belongs, start_position[None, :], 0), axis=1) + offset
    return (occupied, request, slot_group, offset, position)


def block_groups(block_owner, group_count):
    block_count = block_owner.shape[0]
    per_group = block_count // group_count
    entry_ids = jnp.arange(block_count, dtype=jnp.int32)
    hits = block_owner[None, :] == entry_ids[:, None]
    entry = jnp.sum(jnp.where(hits, entry_ids[None, :], 0), axis=1)
    return entry // per_group


def lookup(values, wanted):
    hits = jnp.arange(values.shape[0], dtype=jnp.int32) == wanted
    return jnp.sum(jnp.where(hits, values, 0))


def rotate(vectors, position):
    half_width = vectors.shape[-1] // 2
    pair_ids = jnp.arange(half_width, dtype=jnp.float32)
    frequency = jnp.exp(pair_ids * (-2.0 * math.log(10000.0) / vectors.shape[-1]))
    angles = position.astype(jnp.float32)[:, None] * frequency[None, :]
    cosine = jnp.cos(angles)[:, None, :]
    sine_part = jnp.sin(angles)[:, None, :]
    lower = vectors[..., :half_width]
    upper = vectors[..., half_width:]
    return jnp.concatenate(
        [lower * cosine - upper * sine_part, upper * cosine + lower * sine_part], axis=-1
    )


def layer_norm(values):
    row_mean = jnp.mean(values, axis=-1, keepdims=True)
    centered = values - row_mean
    row_var = jnp.mean(centered * centered, axis=-1, keepdims=True)
    return centered * lax.rsqrt(row_var + EPS)


def block_partial(queries, key_rows, value_rows, allowed):
    score_scale = queries.shape[-1] ** (-0.5)
    scores = (
        jnp.einsum("shd,khd->hsk", queries, key_rows, preferred_element_type=jnp.float32)
        * score_scale
    )
    scores = jnp.where(allowed[None], scores, NEG)
    row_max = jnp.max(scores, axis=-1)
    weights = jnp.where(allowed[None], jnp.exp(scores - row_max[..., None]), 0.0)
    weight_sum = jnp.sum(weights, axis=-1)
    present = jnp.any(allowed, axis=-1)[None, :]
    safe_sum = jnp.where(present, weight_sum, 1.0)
    mixture = jnp.einsum(
        "hsk,khd->shd", weights.astype(jnp.bfloat16), value_rows, preferred_element_type=jnp.float32
    )
    normalized = (mixture / jnp.transpose(safe_sum)[:, :, None]).astype(jnp.bfloat16)
    log_sum = jnp.where(present, row_max + jnp.log(safe_sum), NEG)
    return (normalized, jnp.transpose(log_sum))


def combine(merged, partial_out, partial_lse):
    weighted, running_max, weight_sum = merged
    new_max = jnp.maximum(running_max, partial_lse)
    old_scale = jnp.exp(running_max - new_max)
    new_scale = jnp.exp(partial_lse - new_max)
    weighted = (
        weighted * old_scale[..., None] + partial_out.astype(jnp.float32) * new_scale[..., None]
    )
    return (weighted, new_max, weight_sum * old_scale + new_scale)


def feed_forward(residual_rows, gate_up_weight, down_weight):
    full_rows = lax.all_gather(residual_rows, "mdl", axis=1, tiled=True)
    normed = layer_norm(full_rows.astype(jnp.float32)).astype(jnp.bfloat16)
    gate_up = jnp.einsum("sd,dtf->stf", normed, gate_up_weight, preferred_element_type=jnp.float32)
    hidden = (jax.nn.silu(gate_up[:, 0]) * gate_up[:, 1]).astype(jnp.bfloat16)
    partial_sums = jnp.dot(hidden, down_weight, preferred_element_type=jnp.float32)
    return lax.psum_scatter(
        partial_sums.astype(jnp.bfloat16), "mdl", scatter_dimension=1, tiled=True
    ).astype(jnp.float32)


def local(
    tokens,
    prefix_cache,
    qkv_weight,
    out_weight,
    gate_up_weight,
    down_weight,
    lengths,
    placement,
    request_group,
    block_owner,
    start_position,
):
    capacity = tokens.shape[0]
    head_width = out_weight.shape[0]
    head_count = head_width // HD
    block_rows = prefix_cache.shape[0]
    device = lax.axis_index("req")
    occupied, request, slot_group, offset, position = slot_table(
        lengths, placement, request_group, start_position, device, capacity
    )
    gathered = lax.all_gather(tokens, "mdl", axis=1, tiled=True)
    normed = layer_norm(gathered.astype(jnp.float32)).astype(jnp.bfloat16)
    projected = jnp.einsum("sd,dtc->stc", normed, qkv_weight, preferred_element_type=jnp.float32)
    queries = rotate(projected[:, 0].reshape(capacity, head_count, HD), position).astype(
        jnp.bfloat16
    )
    key_rows = rotate(projected[:, 1].reshape(capacity, head_count, HD), position).astype(
        jnp.bfloat16
    )
    value_rows = projected[:, 2].reshape(capacity, head_count, HD).astype(jnp.bfloat16)
    group_table = block_groups(block_owner, G)
    start_state = (
        jnp.zeros((capacity, head_count, HD), jnp.float32),
        jnp.full((capacity, head_count), NEG, jnp.float32),
        jnp.zeros((capacity, head_count), jnp.float32),
    )
    merged = start_state
    arrived = lax.all_gather(prefix_cache, "req", axis=0, tiled=True)
    block_count = arrived.shape[0] // block_rows
    blocks = arrived.reshape(block_count, block_rows, 2, head_count, HD)

    def over_blocks(running, element):
        block, block_index = element
        block_group = lookup(group_table, block_index)
        allowed = jnp.broadcast_to((slot_group == block_group)[:, None], (capacity, block_rows))
        partial_out, partial_lse = block_partial(queries, block[:, 0], block[:, 1], allowed)
        return (combine(running, partial_out, partial_lse), None)

    merged, unused = lax.scan(
        over_blocks, merged, (blocks, jnp.arange(block_count, dtype=jnp.int32))
    )
    causal = (
        occupied[:, None]
        & occupied[None, :]
        & (request[:, None] == request[None, :])
        & (offset[None, :] <= offset[:, None])
    )
    partial_out, partial_lse = block_partial(queries, key_rows, value_rows, causal)
    weighted, running_max, weight_sum = combine(merged, partial_out, partial_lse)
    attention = (
        (weighted / weight_sum[..., None]).reshape(capacity, head_width).astype(jnp.bfloat16)
    )
    head_terms = jnp.dot(attention, out_weight, preferred_element_type=jnp.float32)
    residual = (
        tokens.astype(jnp.float32)
        + lax.psum_scatter(
            head_terms.astype(jnp.bfloat16), "mdl", scatter_dimension=1, tiled=True
        ).astype(jnp.float32)
    ).astype(jnp.bfloat16)
    finished = residual.astype(jnp.float32) + feed_forward(residual, gate_up_weight, down_weight)
    return jnp.where(occupied[:, None], finished, 0.0).astype(jnp.bfloat16)


def solution(mesh):
    in_specs = (
        P("req", "mdl"),
        P("req", None, "mdl"),
        P(None, None, "mdl"),
        P("mdl", None),
        P(None, None, "mdl"),
        P("mdl", None),
        P(),
        P(),
        P(),
        P(),
        P(),
    )
    out_specs = P("req", "mdl")
    return jax.shard_map(local, mesh=mesh, in_specs=in_specs, out_specs=out_specs, check_vma=False)
```

profile of v0, /device:TPU:8, one launch (start us, length us, event | category | flops | bytes accessed | tf_op | source)
XLA Modules:
  0.0 526.2 jit_solution(17898964725796724855)
XLA Ops:
  15.4 22.5 %all-gather.6.cloned.1.call-done = bf16[256,2048]{1,0:T(8,128)(2,1)} async-done(((bf16[256,256]{1,0:T(8,128)(2,1)}), bf16[256,2048]{1,0:T(8,128)(2,1)}) %all-gather.6.cloned.1.call-update) | async-done | bytes 1048592 | tf_op jit(solution)/shard_map/all_gather | solution.py:135
  38.0 1.5 convert_reduce_fusion.1
  39.5 1.6 fusion.26
  41.2 1.5 fusion.37
  45.9 1.7 fusion.75
  47.6 1.7 copy.66
  49.3 1.7 copy.67
  51.0 1.7 copy.65
  57.2 123.7 %all-gather.4.cloned.1.call-done = bf16[16384,2,256]{2,1,0:T(2,128)(2,1)} async-done(((bf16[512,2,256]{2,1,0:T(2,128)(2,1)}), bf16[16384,2,256]{2,1,0:T(2,128)(2,1)}) %all-gather.4.cloned.1.call-update) | async-done | bytes 16777232 | tf_op jit(solution)/shard_map/all_gather | solution.py:152
  180.9 41.4 %reshape.208 = bf16[32,512,2,2,128]{4,3,2,1,0:T(2,128)(2,1)} reshape(bf16[16384,2,256]{2,1,0:T(2,128)(2,1)} %all-gather.4.cloned.1.call-done) | data formatting | bytes 33554432 | tf_op jit(solution)/shard_map/reshape | solution.py:154
  222.4 188.9 %while.15 = (s32[]{:T(128)}, f32[256,2,128]{0,2,1:T(8,128)}, f32[256,2]{0,1:T(2,128)S(1)}, f32[256,2]{0,1:T(2,128)S(1)}, s32[32]{0:T(128)S(1)}, /*index=5*/s32[3...) while((s32[]{:T(128)}, f32[256,2,128]{0,2,1:T(8,128)}, ...), condition=%wide.region_13.14_spmd.clone, body=%wide.region_8.0_spmd.clone.sunk | while | flops 137171552 | bytes 8558420 | solution.py:163
  225.1 1.5 constant_dynamic-slice_fusion.2
  231.0 1.5 constant_dynamic-slice_fusion.2
  236.9 1.5 constant_dynamic-slice_fusion.2
  242.9 1.5 constant_dynamic-slice_fusion.2
  248.8 1.5 constant_dynamic-slice_fusion.2
  254.7 1.5 constant_dynamic-slice_fusion.2
  266.5 1.5 constant_dynamic-slice_fusion.2
  272.4 1.5 constant_dynamic-slice_fusion.2
  278.3 1.5 constant_dynamic-slice_fusion.2
  284.2 1.5 constant_dynamic-slice_fusion.2
  290.1 1.5 constant_dynamic-slice_fusion.2
  296.0 1.5 constant_dynamic-slice_fusion.2
  414.4 32.8 %reduce-scatter.3.cloned.1.call-done = bf16[256,256]{1,0:T(8,128)(2,1)} async-done(((bf16[256,2048]{1,0:T(8,128)(2,1)}), bf16[256,256]{1,0:T(8,128)(2,1)}) %reduce-scatter.3.cloned.1.call-update) | async-done | bytes 131088 | tf_op jit(solution)/shard_map/reduce_scatter | solution.py:180
  447.2 1.6 add_convert_fusion
  448.9 24.9 %all-gather.8.cloned.1.call-done = bf16[256,2048]{1,0:T(8,128)(2,1)} async-done(((bf16[256,256]{1,0:T(8,128)(2,1)}), bf16[256,2048]{1,0:T(8,128)(2,1)}) %all-gather.8.cloned.1.call-update) | async-done | bytes 1048592 | tf_op jit(solution)/shard_map/all_gather | solution.py:104
  473.7 1.5 convert_reduce_fusion
  475.3 1.6 fusion.24
  476.9 3.7 fusion.18
  480.6 1.7 convolution_convert_fusion
  482.4 35.6 %reduce-scatter.5.cloned.1.call-done = bf16[256,256]{1,0:T(8,128)(2,1)} async-done(((bf16[256,2048]{1,0:T(8,128)(2,1)}), bf16[256,256]{1,0:T(8,128)(2,1)}) %reduce-scatter.5.cloned.1.call-update) | async-done | bytes 131088 | tf_op jit(solution)/shard_map/reduce_scatter | solution.py:109
  518.0 1.7 select_convert_fusion
  (537 shorter events, 189.1 us)
Async XLA Ops:
  6.5 34.6 %copy-start = (bf16[2048,3,256]{2,0,1:T(8,128)(2,1)S(1)}, bf16[2048,3,256]{2,0,1:T(8,128)(2,1)}, u32[]{:S(2)}) copy-start(bf16[2048,3,256]{2,0,1:T(8,128)(2,1)} %param.15) | copy-start | bytes 9437188
  6.5 31.4 %all-gather.6.cloned.1.call-start = ((), (), s32[]{:S(2)}) async-start(), calls=%async_computation.3 | async-start | bytes 1179648 | tf_op jit(solution)/shard_map/all_gather | solution.py:135
  7.3 173.7 %all-gather.4.cloned.1.call-start = ((), (), s32[]{:S(2)}) async-start(), calls=%async_computation.2 | async-start | bytes 17301504 | tf_op jit(solution)/shard_map/all_gather | solution.py:152
  8.0 439.2 %reduce-scatter.3.cloned.1.call-start = ((), (), s32[]{:S(2)}) async-start(), calls=%async_computation.4 | async-start | bytes 1179648 | tf_op jit(solution)/shard_map/reduce_scatter | solution.py:180
  38.0 3.2 copy-start.1
  52.8 4.4 copy-start.9
  57.2 165.1 %copy-start.14 = (s32[32]{0:T(128)S(1)}, s32[32]{0:T(128)}, u32[]{:S(2)}) copy-start(s32[32]{0:T(128)} %and_select_fusion) | copy-start | bytes 388
  222.4 189.0 %copy-start.10 = (pred[256]{0:T(512)(128)(4,1)S(1)}, pred[256]{0:T(512)(128)(4,1)}, u32[]{:S(2)}) copy-start(pred[256]{0:T(512)(128)(4,1)} %get-tuple-element.157) | copy-start | bytes 772
  222.4 189.0 %copy-start.6 = (pred[256,256]{0,1:T(8,128)(4,1)S(1)}, pred[256,256]{0,1:T(8,128)(4,1)}, u32[]{:S(2)}) copy-start(pred[256,256]{0,1:T(8,128)(4,1)} %copy.53) | copy-start | bytes 196612
  222.4 189.0 %copy-start.8 = (bf16[256,1,256]{0,2,1:T(8,128)(2,1)S(1)}, bf16[256,1,256]{0,2,1:T(8,128)(2,1)}, u32[]{:S(2)}) copy-start(bf16[256,1,256]{0,2,1:T(8,128)(2,1)} %slice.71) | copy-start | bytes 393220
  225.1 2.1 copy-start.12
  231.0 2.1 copy-start.12
  236.9 2.1 copy-start.12
  242.8 2.1 copy-start.12
  266.5 2.1 copy-start.12
  272.4 2.1 copy-start.12
  278.3 2.1 copy-start.12
  284.2 2.1 copy-start.12
  290.1 2.1 copy-start.12
  296.0 2.1 copy-start.12
  301.9 2.1 copy-start.12
  319.6 2.1 copy-start.12
  325.5 2.1 copy-start.12
  331.4 2.1 copy-start.12
  337.3 2.1 copy-start.12
  343.2 2.1 copy-start.12
  412.8 34.4 %copy-start.7 = (bf16[256,256]{1,0:T(8,128)(2,1)S(1)}, bf16[256,256]{1,0:T(8,128)(2,1)}, u32[]{:S(2)}) copy-start(bf16[256,256]{1,0:T(8,128)(2,1)} %param.13) | copy-start | bytes 393220
  414.3 59.4 %all-gather.8.cloned.1.call-start = ((), (), s32[]{:S(2)}) async-start(), calls=%async_computation.5 | async-start | bytes 1179648 | tf_op jit(solution)/shard_map/all_gather | solution.py:104
  448.8 69.2 %reduce-scatter.5.cloned.1.call-start = ((), (), s32[]{:S(2)}) async-start(), calls=%async_computation.6 | async-start | bytes 1179648 | tf_op jit(solution)/shard_map/reduce_scatter | solution.py:109
  473.7 3.2 copy-start.2
  476.9 3.7 copy-start.11
  480.6 37.4 %copy-start.4 = (bf16[256,256]{1,0:T(8,128)(2,1)S(1)}, bf16[256,256]{1,0:T(8,128)(2,1)}, u32[]{:S(2)}) copy-start(bf16[256,256]{1,0:T(8,128)(2,1)} %add_convert_fusion) | copy-start | bytes 393220
  (50 other events, 58.0 us)
Sparse Core Ops, SparseCore 0:
  9.2 28.7 all-gather.5
  40.6 140.3 all-gather.3
  414.4 32.7 reduce-scatter.2
  448.9 24.7 all-gather.7
  482.5 35.4 reduce-scatter.4
where the time goes:
time: 529 us; the launch traced here: 526 us
  waiting for transfers between devices  241 us (46%)
  local copies, waits for them, and re-layouts  145 us (27%)
  other arithmetic  91.8 us (17%)
  matrix products  32.9 us (6%)
  between operations  13.4 us (3%)
    all_gather x1, waiting for transfers between devices, local(): arrived = lax.all_gather(prefix_cache, 'req', axis=0, tiled=True)  124 us
    dynamic_slice x96, local copies, waits for them, and re-layouts, local(): lax.scan(over_blocks, merged, (blocks, jnp.arange(block_count, dtype=jnp....  69.9 us
    reduce_sum x32, other arithmetic, lookup(): return jnp.sum(jnp.where(hits, values, 0))  42 us
    reshape x1, local copies, waits for them, and re-layouts, local(): blocks = arrived.reshape(block_count, block_rows, 2, head_count, HD)  41.4 us
    reduce_scatter x1, waiting for transfers between devices, feed_forward(): lax.psum_scatter(partial_sums.astype(jnp.bfloat16), 'mdl', scatter_dimens...  35.6 us
    reduce_scatter x1, waiting for transfers between devices, local(): lax.psum_scatter(head_terms.astype(jnp.bfloat16), 'mdl', scatter_dimensio...  32.8 us
    all_gather x1, waiting for transfers between devices, feed_forward(): full_rows = lax.all_gather(residual_rows, 'mdl', axis=1, tiled=True)  24.9 us
    all_gather x1, waiting for transfers between devices, local(): gathered = lax.all_gather(tokens, 'mdl', axis=1, tiled=True)  22.5 us
  transfers between devices with their start and end apart: 5, of which 5 were waited for; matrix products, arithmetic and copies ran while one was open for 5% of the time, Pallas kernels for 0%

commit v1 on v0

--- a/solution.py
+++ b/solution.py
@@ -1,3 +1,4 @@
+import functools
 import math
 import jax
 import jax.numpy as jnp
@@ -8,6 +9,22 @@
 G = 4
 NEG = -1e30
 EPS = 1e-05
+
+
+def arrange_values(sheet, mesh_ax):
+    sides = lax.axis_size(mesh_ax)
+    r_now = list(map(lambda p: (p - 1, p), range(1, sides)))
+    prior = r_now + [(sides - 1, 0)]
+    near = sheet
+    in_order = [near]
+    for _ in range(sides - 1):
+        near = lax.ppermute(near, axis_name=mesh_ax, perm=prior)
+        in_order += [near]
+    newest = jnp.concatenate([*reversed(in_order)], axis=1)
+    return jnp.roll(newest, (lax.axis_index(mesh_ax) + 1) * near.shape[1], axis=1)
+
+
+use_sides = functools.partial(arrange_values, mesh_ax="mdl")
 
 
 def slot_table(lengths, placement, request_group, start_position, device, capacity):
@@ -132,7 +149,7 @@
     occupied, request, slot_group, offset, position = slot_table(
         lengths, placement, request_group, start_position, device, capacity
     )
-    gathered = lax.all_gather(tokens, "mdl", axis=1, tiled=True)
+    gathered = use_sides(tokens)
     normed = layer_norm(gathered.astype(jnp.float32)).astype(jnp.bfloat16)
     projected = jnp.einsum("sd,dtc->stc", normed, qkv_weight, preferred_element_type=jnp.float32)
     queries = rotate(projected[:, 0].reshape(capacity, head_count, HD), position).astype(

time: 529 us -> 500 us (0.945)
  waiting for transfers between devices: 241 us -> 208 us
  local copies, waits for them, and re-layouts: 145 us -> 153 us
    all_gather x1, waiting for transfers between devices: 124 us -> 80.7 us  [local(): arrived = lax.all_gather(prefix_cache, 'req', axis=0, tiled=True)]
    ppermute x0 -> x7, waiting for transfers between devices: none -> 33.5 us  [arrange_values(): near = lax.ppermute(near, axis_name=mesh_ax, perm=prior)]
    all_gather x1 -> x0, waiting for transfers between devices: 22.5 us -> none  [local(): gathered = lax.all_gather(tokens, 'mdl', axis=1, tiled=True)]
    unnamed x30 -> x51, local copies, waits for them, and re-layouts: 7.08 us -> 15.9 us
  transfers between devices with their start and end apart: 5 -> 11, of which waited for: 5 -> 11; matrix products, arithmetic and copies ran while one was open for 5% -> 6% of each run, Pallas kernels for 0% -> 0%
where the time goes in v1:
time: 500 us; the launch traced here: 497 us
  waiting for transfers between devices  208 us (42%)
  local copies, waits for them, and re-layouts  153 us (31%)
  other arithmetic  88 us (18%)
  matrix products  32 us (6%)
  between operations  13.5 us (3%)
    all_gather x1, waiting for transfers between devices, local(): arrived = lax.all_gather(prefix_cache, 'req', axis=0, tiled=True)  80.7 us
    dynamic_slice x96, local copies, waits for them, and re-layouts, local(): lax.scan(over_blocks, merged, (blocks, jnp.arange(block_count, dtype=jnp....  69.9 us
    reduce_sum x32, other arithmetic, lookup(): return jnp.sum(jnp.where(hits, values, 0))  42 us
    reshape x1, local copies, waits for them, and re-layouts, local(): blocks = arrived.reshape(block_count, block_rows, 2, head_count, HD)  41.4 us
    reduce_scatter x1, waiting for transfers between devices, feed_forward(): lax.psum_scatter(partial_sums.astype(jnp.bfloat16), 'mdl', scatter_dimens...  35.6 us
    ppermute x7, waiting for transfers between devices, arrange_values(): near = lax.ppermute(near, axis_name=mesh_ax, perm=prior)  33.5 us
    reduce_scatter x1, waiting for transfers between devices, local(): lax.psum_scatter(head_terms.astype(jnp.bfloat16), 'mdl', scatter_dimensio...  32.9 us
    all_gather x1, waiting for transfers between devices, feed_forward(): full_rows = lax.all_gather(residual_rows, 'mdl', axis=1, tiled=True)  25 us
  transfers between devices with their start and end apart: 11, of which 11 were waited for; matrix products, arithmetic and copies ran while one was open for 6% of the time, Pallas kernels for 0%

profile of v1, /device:TPU:8, one launch (start us, length us, event | category | flops | bytes accessed | tf_op | source)
XLA Modules:
  0.0 497.3 jit_solution(1443835508242681260)
XLA Ops:
  8.1 5.0 %collective-permute-done = bf16[256,256]{1,0:T(8,128)(2,1)S(1)} collective-permute-done((bf16[256,256]{1,0:T(8,128)(2,1)}, bf16[256,256]{1,0:T(8,128)(2,1)S(1)}, u32[]{:S(2)}, u32[]{:S(2)}) %collective-permute-start) | collective-permute-done | bytes 131104 | tf_op jit(solution)/shard_map/ppermute | solution.py:21
  15.6 3.1 collective-permute-done.1
  18.8 5.6 %collective-permute-done.2 = bf16[256,256]{1,0:T(8,128)(2,1)S(1)} collective-permute-done((bf16[256,256]{1,0:T(8,128)(2,1)S(1)}, bf16[256,256]{1,0:T(8,128)(2,1)S(1)}, u32[]{:S(2)}, u32[]{:S(2)}) %collective-permute-start.2) | collective-permute-done | bytes 131104 | tf_op jit(solution)/shard_map/ppermute | solution.py:21
  25.7 4.3 collective-permute-done.3
  31.4 4.9 collective-permute-done.4
  37.4 4.8 collective-permute-done.5
  42.3 5.8 %collective-permute-done.6 = bf16[256,256]{1,0:T(8,128)(2,1)S(1)} collective-permute-done((bf16[256,256]{1,0:T(8,128)(2,1)}, bf16[256,256]{1,0:T(8,128)(2,1)S(1)}, u32[]{:S(2)}, u32[]{:S(2)}) %collective-permute-start.6) | collective-permute-done | bytes 131104 | tf_op jit(solution)/shard_map/ppermute | solution.py:21
  56.3 1.5 fusion.37
  59.9 1.7 copy.68
  61.6 1.7 fusion.77
  63.3 1.7 copy.66
  65.0 1.7 copy.67
  66.8 1.8 copy.65
  71.3 80.7 %all-gather.3.cloned.1.call-done = bf16[16384,2,256]{2,1,0:T(2,128)(2,1)} async-done(((bf16[512,2,256]{2,1,0:T(2,128)(2,1)}), bf16[16384,2,256]{2,1,0:T(2,128)(2,1)}) %all-gather.3.cloned.1.call-update) | async-done | bytes 16777232 | tf_op jit(solution)/shard_map/all_gather | solution.py:169
  152.0 41.4 %reshape.208 = bf16[32,512,2,2,128]{4,3,2,1,0:T(2,128)(2,1)} reshape(bf16[16384,2,256]{2,1,0:T(2,128)(2,1)} %all-gather.3.cloned.1.call-done) | data formatting | bytes 33554432 | tf_op jit(solution)/shard_map/reshape | solution.py:171
  193.4 188.9 %while.15 = (s32[]{:T(128)}, f32[256,2,128]{0,2,1:T(8,128)}, f32[256,2]{0,1:T(2,128)S(1)}, f32[256,2]{0,1:T(2,128)S(1)}, s32[32]{0:T(128)S(1)}, /*index=5*/s32[3...) while((s32[]{:T(128)}, f32[256,2,128]{0,2,1:T(8,128)}, ...), condition=%wide.region_13.14_spmd.clone, body=%wide.region_8.13_spmd.clone.sunk | while | flops 137171552 | bytes 8558420 | solution.py:180
  202.1 1.5 constant_dynamic-slice_fusion.2
  208.0 1.5 constant_dynamic-slice_fusion.2
  213.9 1.5 constant_dynamic-slice_fusion.2
  225.7 1.5 constant_dynamic-slice_fusion.2
  231.6 1.5 constant_dynamic-slice_fusion.2
  237.5 1.5 constant_dynamic-slice_fusion.2
  382.3 1.5 fusion.35
  385.4 32.9 %reduce-scatter.3.cloned.1.call-done = bf16[256,256]{1,0:T(8,128)(2,1)} async-done(((bf16[256,2048]{1,0:T(8,128)(2,1)}), bf16[256,256]{1,0:T(8,128)(2,1)}) %reduce-scatter.3.cloned.1.call-update) | async-done | bytes 131088 | tf_op jit(solution)/shard_map/reduce_scatter | solution.py:197
  418.2 1.6 add_convert_fusion
  419.9 25.0 %all-gather.5.cloned.1.call-done = bf16[256,2048]{1,0:T(8,128)(2,1)} async-done(((bf16[256,256]{1,0:T(8,128)(2,1)}), bf16[256,2048]{1,0:T(8,128)(2,1)}) %all-gather.5.cloned.1.call-update) | async-done | bytes 1048592 | tf_op jit(solution)/shard_map/all_gather | solution.py:121
  444.9 1.5 convert_reduce_fusion
  446.4 1.6 fusion.24
  448.1 3.7 fusion.18
  451.8 1.7 convolution_convert_fusion
  453.5 35.6 %reduce-scatter.5.cloned.1.call-done = bf16[256,256]{1,0:T(8,128)(2,1)} async-done(((bf16[256,2048]{1,0:T(8,128)(2,1)}), bf16[256,256]{1,0:T(8,128)(2,1)}) %reduce-scatter.5.cloned.1.call-update) | async-done | bytes 131088 | tf_op jit(solution)/shard_map/reduce_scatter | solution.py:126
  489.1 1.7 select_convert_fusion
  (570 shorter events, 200.7 us)
Async XLA Ops:
  6.5 49.8 %copy-start = (bf16[2048,3,256]{2,0,1:T(8,128)(2,1)S(1)}, bf16[2048,3,256]{2,0,1:T(8,128)(2,1)}, u32[]{:S(2)}) copy-start(bf16[2048,3,256]{2,0,1:T(8,128)(2,1)} %param.15) | copy-start | bytes 9437188
  6.5 47.1 %copy-start.3 = (bf16[256,256]{1,0:T(8,128)(2,1)S(1)}, bf16[256,256]{1,0:T(8,128)(2,1)}, u32[]{:S(2)}) copy-start(bf16[256,256]{1,0:T(8,128)(2,1)} %param.13) | copy-start | bytes 393220
  6.5 145.5 %all-gather.3.cloned.1.call-start = ((), (), s32[]{:S(2)}) async-start(), calls=%async_computation.2 | async-start | bytes 17301504 | tf_op jit(solution)/shard_map/all_gather | solution.py:169
  7.3 411.0 %reduce-scatter.3.cloned.1.call-start = ((), (), s32[]{:S(2)}) async-start(), calls=%async_computation.3 | async-start | bytes 1179648 | tf_op jit(solution)/shard_map/reduce_scatter | solution.py:197
  7.3 5.8 %collective-permute-start = (bf16[256,256]{1,0:T(8,128)(2,1)}, bf16[256,256]{1,0:T(8,128)(2,1)S(1)}, u32[]{:S(2)}, u32[]{:S(2)}) collective-permute-start(bf16[256,256]{1,0:T(8,128)(2,1)} %param.13), channel_id=1, source_target_pairs={{0,1},{1,2},{2,3},{3,4},{4,5},{5,6},{6,7},{7,0},{8,9},{9,10},{10,1... | collective-permute-start | bytes 393224 | tf_op jit(solution)/shard_map/ppermute | solution.py:21
  13.1 11.2 %copy-start.6 = (bf16[256,256]{1,0:T(8,128)(2,1)}, bf16[256,256]{1,0:T(8,128)(2,1)S(1)}, u32[]{:S(2)}) copy-start(bf16[256,256]{1,0:T(8,128)(2,1)S(1)} %collective-permute-done) | copy-start | bytes 393220
  13.1 5.6 %collective-permute-start.1 = (bf16[256,256]{1,0:T(8,128)(2,1)S(1)}, bf16[256,256]{1,0:T(8,128)(2,1)S(1)}, u32[]{:S(2)}, u32[]{:S(2)}) collective-permute-start(bf16[256,256]{1,0:T(8,128)(2,1)S(1)} %collective-permute-done), channel_id=1, source_target_pairs={{0,1},{1,2},{2,3},{3,4},{4,5},{5,6},{6,7},{7,0},{8,9},{9,10},{10,1... | collective-permute-start | bytes 393224 | tf_op jit(solution)/shard_map/ppermute | solution.py:21
  18.7 5.6 %copy-start.8 = (bf16[256,256]{1,0:T(8,128)(2,1)}, bf16[256,256]{1,0:T(8,128)(2,1)S(1)}, u32[]{:S(2)}) copy-start(bf16[256,256]{1,0:T(8,128)(2,1)S(1)} %collective-permute-done.1) | copy-start | bytes 393220
  18.7 5.6 %collective-permute-start.2 = (bf16[256,256]{1,0:T(8,128)(2,1)S(1)}, bf16[256,256]{1,0:T(8,128)(2,1)S(1)}, u32[]{:S(2)}, u32[]{:S(2)}) collective-permute-start(bf16[256,256]{1,0:T(8,128)(2,1)S(1)} %collective-permute-done.1), channel_id=1, source_target_pairs={{0,1},{1,2},{2,3},{3,4},{4,5},{5,6},{6,7},{7,0},{8,9},{9,10},{10,1... | collective-permute-start | bytes 393224 | tf_op jit(solution)/shard_map/ppermute | solution.py:21
  24.3 5.6 %collective-permute-start.3 = (bf16[256,256]{1,0:T(8,128)(2,1)S(1)}, bf16[256,256]{1,0:T(8,128)(2,1)S(1)}, u32[]{:S(2)}, u32[]{:S(2)}) collective-permute-start(bf16[256,256]{1,0:T(8,128)(2,1)S(1)} %collective-permute-done.2), channel_id=1, source_target_pairs={{0,1},{1,2},{2,3},{3,4},{4,5},{5,6},{6,7},{7,0},{8,9},{9,10},{10,1... | collective-permute-start | bytes 393224 | tf_op jit(solution)/shard_map/ppermute | solution.py:21
  30.6 5.7 %collective-permute-start.4 = (bf16[256,256]{1,0:T(8,128)(2,1)S(1)}, bf16[256,256]{1,0:T(8,128)(2,1)}, u32[]{:S(2)}, u32[]{:S(2)}) collective-permute-start(bf16[256,256]{1,0:T(8,128)(2,1)S(1)} %collective-permute-done.3), channel_id=1, source_target_pairs={{0,1},{1,2},{2,3},{3,4},{4,5},{5,6},{6,7},{7,0},{8,9},{9,10},{10,1... | collective-permute-start | bytes 393224 | tf_op jit(solution)/shard_map/ppermute | solution.py:21
  36.3 5.9 %collective-permute-start.5 = (bf16[256,256]{1,0:T(8,128)(2,1)}, bf16[256,256]{1,0:T(8,128)(2,1)}, u32[]{:S(2)}, u32[]{:S(2)}) collective-permute-start(bf16[256,256]{1,0:T(8,128)(2,1)} %collective-permute-done.4), channel_id=1, source_target_pairs={{0,1},{1,2},{2,3},{3,4},{4,5},{5,6},{6,7},{7,0},{8,9},{9,10},{10,1... | collective-permute-start | bytes 393224 | tf_op jit(solution)/shard_map/ppermute | solution.py:21
  36.5 18.9 %copy-start.13 = (bf16[256,256]{1,0:T(8,128)(2,1)S(1)}, bf16[256,256]{1,0:T(8,128)(2,1)}, u32[]{:S(2)}) copy-start(bf16[256,256]{1,0:T(8,128)(2,1)} %copy-done.12) | copy-start | bytes 393220
  36.6 19.0 %copy-start.11 = (bf16[256,256]{1,0:T(8,128)(2,1)S(1)}, bf16[256,256]{1,0:T(8,128)(2,1)}, u32[]{:S(2)}) copy-start(bf16[256,256]{1,0:T(8,128)(2,1)} %copy-done.10) | copy-start | bytes 393220
  36.6 19.0 %copy-start.9 = (bf16[256,256]{1,0:T(8,128)(2,1)S(1)}, bf16[256,256]{1,0:T(8,128)(2,1)}, u32[]{:S(2)}) copy-start(bf16[256,256]{1,0:T(8,128)(2,1)} %copy-done.8) | copy-start | bytes 393220
  36.6 19.0 %copy-start.7 = (bf16[256,256]{1,0:T(8,128)(2,1)S(1)}, bf16[256,256]{1,0:T(8,128)(2,1)}, u32[]{:S(2)}) copy-start(bf16[256,256]{1,0:T(8,128)(2,1)} %copy-done.6) | copy-start | bytes 393220
  42.2 5.8 %collective-permute-start.6 = (bf16[256,256]{1,0:T(8,128)(2,1)}, bf16[256,256]{1,0:T(8,128)(2,1)S(1)}, u32[]{:S(2)}, u32[]{:S(2)}) collective-permute-start(bf16[256,256]{1,0:T(8,128)(2,1)} %collective-permute-done.5), channel_id=1, source_target_pairs={{0,1},{1,2},{2,3},{3,4},{4,5},{5,6},{6,7},{7,0},{8,9},{9,10},{10,1... | collective-permute-start | bytes 393224 | tf_op jit(solution)/shard_map/ppermute | solution.py:21
  66.8 4.5 copy-start.14
  225.7 2.1 copy-start.16
  231.6 2.1 copy-start.16
  237.5 2.1 copy-start.16
  243.4 2.1 copy-start.16
  249.3 2.1 copy-start.16
  255.2 2.1 copy-start.16
  261.1 2.1 copy-start.16
  278.8 2.1 copy-start.16
  284.7 2.1 copy-start.16
  385.3 59.6 %all-gather.5.cloned.1.call-start = ((), (), s32[]{:S(2)}) async-start(), calls=%async_computation.4 | async-start | bytes 1179648 | tf_op jit(solution)/shard_map/all_gather | solution.py:121
  419.8 69.3 %reduce-scatter.5.cloned.1.call-start = ((), (), s32[]{:S(2)}) async-start(), calls=%async_computation.5 | async-start | bytes 1179648 | tf_op jit(solution)/shard_map/reduce_scatter | solution.py:126
  444.9 3.2 copy-start.1
  448.1 3.7 copy-start.15
  451.8 37.3 %copy-start.4 = (bf16[256,256]{1,0:T(8,128)(2,1)S(1)}, bf16[256,256]{1,0:T(8,128)(2,1)}, u32[]{:S(2)}) copy-start(bf16[256,256]{1,0:T(8,128)(2,1)} %add_convert_fusion) | copy-start | bytes 393220
  (59 other events, 74.6 us)
Sparse Core Ops, SparseCore 0:
  9.9 142.0 all-gather.2
  385.4 32.7 reduce-scatter.2
  420.1 24.7 all-gather.4
  453.7 35.4 reduce-scatter.4
